TPU v7x, 32 devices: a whole 2x2x4 slice. The times are simulated.
32 devices in a mesh: real: 4 (over y, core), sky: 8 (over z, x).
Axes of the slice: x: 2, y: 2, z: 4, core: 2. Of those that a mesh axis runs over, the one named last changes fastest.
Arguments:
- potential_stock: bfloat16 [8, 256, 16384], P('real', 'sky'), may hold values from -6 to 6
- plane_pick: int32 [4], replicated, may hold values from 0 to 7, as said below
- col_shift: int32 [4, 4], P('real'), may hold values from 0 to 16383
- mirror: int32 [4, 4], P('real'), may hold values from 0 to 1
- subcell: int32 [32, 16], P('sky'), may hold values from 0 to 15
- lens_weight: float32 [4], replicated, may hold values from 0.02 to 0.08
Outputs:
- deflect: float32 [2, 4, 256, 2048], P(None, 'real', 'sky')
- distort: float32 [4, 4, 256, 2048], P(None, 'real', 'sky')
Inputs may be any that keep to these rules, and one draw needn't show every extreme that they name: `plane_pick`: the 4 entries are distinct stored entries; entry q is held by the realization group q // 2.
All inputs are finite; a program needn't handle non-finite values.
Results may differ from a plain program's by a relative error of at most 0.0003.
Values may be sent and summed in bfloat16 or wider, within the bound.
A program may use at most 64 MiB of HBM per device.

v0:
```python
import jax
import jax.numpy as jnp
from jax import lax
from jax.sharding import PartitionSpec as P

PLANES = 4
SUB = 4
TILE_R = 8
TILE_C = 128
first_coef = (1.0 / 12.0, -8.0 / 12.0, 0.0, 8.0 / 12.0, -1.0 / 12.0)
second_coef = (-1.0 / 12.0, 16.0 / 12.0, -30.0 / 12.0, 16.0 / 12.0, -1.0 / 12.0)


def extended_2(x, sides, width):
    for axis, dim in sides:
        peers, length = (lax.axis_size(axis), x.shape[dim])
        up = [(i, (i + 1) % peers) for i in range(peers)]
        down = [(j, i) for i, j in up]
        last = lax.slice_in_dim(x, length - width, length, axis=dim)
        first = lax.slice_in_dim(x, 0, width, axis=dim)
        before = lax.ppermute(last, axis, up)
        after = lax.ppermute(first, axis, down)
        x = jnp.concatenate([before, x, after], axis=dim)
    return x


def spread(value, axis, source):
    kept = jnp.where(lax.axis_index(axis) == source, value, 0).astype(value.dtype)
    return lax.psum(kept, axis)


def cubic_weights(frac):
    sq = frac * frac
    cube = sq * frac
    return (
        (-cube + 2.0 * sq - frac) * 0.5,
        (3.0 * cube - 5.0 * sq + 2.0) * 0.5,
        (-3.0 * cube + 4.0 * sq + frac) * 0.5,
        (cube - sq) * 0.5,
    )


def tap_weights(subcell):
    frac_x = ((subcell % SUB).astype(jnp.float32) + 0.5) / SUB
    frac_y = ((subcell // SUB).astype(jnp.float32) + 0.5) / SUB
    weights_x = tuple((w[:, None, :, None] for w in cubic_weights(frac_x)))
    weights_y = tuple((w[:, None, :, None] for w in cubic_weights(frac_y)))
    return (weights_x, weights_y)


def derivatives(tile):
    nrows = tile.shape[0] - 5
    ncols = tile.shape[1] - 5

    def window(drow, dcol):
        return tile[3 + drow : 3 + drow + nrows, 3 + dcol : 3 + dcol + ncols]

    grad_x = sum((first_coef[q] * window(0, q - 2) for q in range(5) if q != 2))
    grad_y = sum((first_coef[q] * window(q - 2, 0) for q in range(5) if q != 2))
    hess_xx = sum((second_coef[q] * window(0, q - 2) for q in range(5)))
    hess_yy = sum((second_coef[q] * window(q - 2, 0) for q in range(5)))
    hess_xy = sum(
        (
            first_coef[p] * first_coef[q] * window(p - 2, q - 2)
            for p in range(5)
            for q in range(5)
            if p != 2 and q != 2
        )
    )
    return (grad_x, grad_y, hess_xx, hess_yy, hess_xy)


def sample(field, weights_x, weights_y, nrows, ncols):
    total = jnp.zeros((nrows // TILE_R, TILE_R, ncols // TILE_C, TILE_C), jnp.float32)
    for brow in range(4):
        inner = jnp.zeros_like(total)
        for acol in range(4):
            piece = field[brow : brow + nrows, acol : acol + ncols]
            piece = piece.reshape(nrows // TILE_R, TILE_R, ncols // TILE_C, TILE_C)
            inner = inner + weights_x[acol] * piece
        total = total + weights_y[brow] * inner
    return total.reshape(nrows, ncols)


def advance(state, tile, weights_x, weights_y, lens):
    nrows = tile.shape[0] - 8
    ncols = tile.shape[1] - 8
    fields = derivatives(tile.astype(jnp.float32))
    grad_x, grad_y, hess_xx, hess_yy, hess_xy = [
        sample(f, weights_x, weights_y, nrows, ncols) for f in fields
    ]
    shift_x, shift_y, a_11, a_12, a_21, a_22 = state
    shift_x = shift_x + lens * grad_x
    shift_y = shift_y + lens * grad_y
    new_11 = a_11 - lens * (hess_xx * a_11 + hess_xy * a_21)
    new_12 = a_12 - lens * (hess_xx * a_12 + hess_xy * a_22)
    new_21 = a_21 - lens * (hess_xy * a_11 + hess_yy * a_21)
    new_22 = a_22 - lens * (hess_xy * a_12 + hess_yy * a_22)
    return (shift_x, shift_y, new_11, new_12, new_21, new_22)


def cut_columns(band, shift, flip, width):
    flipped = jnp.where(flip == 1, band[..., ::-1], band)
    extended = jnp.concatenate([flipped, flipped[..., : width + 8]], axis=-1)
    start = (shift - 4) % band.shape[-1]
    return lax.dynamic_slice_in_dim(extended, start, width + 8, flipped.ndim - 1)


def add_edges(blocks):
    return extended_2(blocks, (("sky", 1),), 4)


def body(potential_stock, plane_pick, col_shift, mirror, subcell, lens_weight):
    nrows = subcell.shape[0] * TILE_R
    ncols = subcell.shape[1] * TILE_C
    held = potential_stock.shape[0]
    weights_x, weights_y = tap_weights(subcell)
    zeros = jnp.zeros((nrows, ncols), jnp.float32)
    ones = jnp.ones((nrows, ncols), jnp.float32)
    state = (zeros, zeros, ones, zeros, zeros, ones)
    for plane in range(PLANES):
        entry = plane_pick[plane]
        own = lax.dynamic_index_in_dim(potential_stock, entry % held, 0, keepdims=False)
        band = spread(own, "real", entry // held)
        view = add_edges(cut_columns(band, col_shift[0, plane], mirror[0, plane], ncols)[None])[0]
        state = advance(state, view, weights_x, weights_y, lens_weight[plane])
    deflect = jnp.stack([state[0], state[1]])[:, None]
    distort = jnp.stack([state[2], state[3], state[4], state[5]])[:, None]
    return (deflect, distort)


def solution(mesh):
    return jax.shard_map(
        body,
        mesh=mesh,
        in_specs=(
            P("real", "sky", None),
            P(),
            P("real", None),
            P("real", None),
            P("sky", None),
            P(),
        ),
        out_specs=(P(None, "real", "sky", None), P(None, "real", "sky", None)),
        check_vma=False,
    )
```

profile of v0, /device:TPU:0, one launch (start us, length us, event | category | flops | bytes accessed | tf_op | source)
XLA Modules:
  0.0 336.1 jit_solution(15241077179185360147)
XLA Ops:
  7.2 0.0 all-reduce.3.cloned.1.call-start
  7.2 1.4 fusion.436
  18.8 4.3 %select_bitcast_fusion.3 = (bf16[32,16384]{1,0:T(8,128)(2,1)}, bf16[32,16384]{1,0:T(8,128)(2,1)}, bf16[32,16384]{1,0:T(8,128)(2,1)}, bf16[32,16384]{1,0:T(8,128)(2,1)}) fusion(bf16[2,32,16384]{2,1,0:T(8,128)(2,1)} %param.6, s32[]{:T(128)S(6)} %select_n.154, pred[]{:T(512)S(6)} %eq.49, s32[]{:T(128)S(6)} %select_n.164, pred[]{:T(512)S(6)} %eq.52, ...), kind=kLoop, calls=%fused_computation.412 | loop fusion | flops 2097152 | bytes 8388628 | tf_op jit(solution)/shard_map/jit(_where)/select_n | solution.py:28
  23.0 0.0 copy-start.7
  23.0 0.0 all-reduce.3.cloned.1.call-update
  23.1 0.6 copy-done.4
  23.7 0.7 fusion.435
  27.0 0.0 copy-done.5
  27.0 0.7 fusion.434
  30.2 0.0 copy-done.6
  30.2 0.7 fusion.433
  30.9 80.6 %all-reduce.3.cloned.1.call-done = (bf16[32,16384]{1,0:T(8,128)(2,1)}, bf16[32,16384]{1,0:T(8,128)(2,1)}, bf16[32,16384]{1,0:T(8,128)(2,1)}, bf16[32,16384]{1,0:T(8,128)(2,1)}) async-done(((bf16[32,16384]{1,0:T(8,128)(2,1)}, bf16[32,16384]{1,0:T(8,128)(2,1)}, bf16[32,16384]{1,0:T(8,128)(2,1)}, bf16[32,16384]{1,0:T(8,128)(2,1)}), (bf16[32,16384]{1,0:T(8,128)(2,1)}, bf16[32,16384]{1,0:T(8,128)(2,1)}, ...) | async-done | bytes 4194320 | tf_op jit(solution)/shard_map/psum | solution.py:29
  111.5 50.0 %rev.15 = bf16[32,16384]{1,0:T(8,128)(2,1)S(1)} reverse(bf16[32,16384]{1,0:T(8,128)(2,1)} %get-tuple-element.2), dimensions={1} | reverse | bytes 2097152 | tf_op jit(solution)/shard_map/rev | solution.py:103
  161.5 43.2 %rev.14 = bf16[32,16384]{1,0:T(8,128)(2,1)} reverse(bf16[32,16384]{1,0:T(8,128)(2,1)S(1)} %copy-done.3), dimensions={1} | reverse | bytes 2097152 | tf_op jit(solution)/shard_map/rev | solution.py:103
  204.8 1.4 broadcast_select_fusion
  206.2 0.2 fusion.387
  206.5 0.6 fusion.432
  207.1 4.2 %collective-permute-start.7 = (bf16[1,4,2056]{2,1,0:T(4,128)(2,1)}, bf16[1,4,2056]{2,1,0:T(4,128)(2,1)S(1)}, u32[]{:S(2)}, u32[]{:S(2)}) collective-permute-start(bf16[1,4,2056]{2,1,0:T(4,128)(2,1)} %get-tuple-element.60), channel_id=1, source_target_pairs={{1,0},{2,1},{3,2},{4,3},{5,4},{6,5},{7,6},{0,7},{9,8},{10,9},{11,1... | collective-permute-start | bytes 49352 | tf_op jit(solution)/shard_map/ppermute | solution.py:22
  211.3 0.0 collective-permute-start.6
  211.3 0.2 fusion.386
  211.6 0.0 copy-start.1
  211.6 0.6 fusion.431
  212.2 4.7 %collective-permute-start.5 = (bf16[1,4,2056]{2,1,0:T(4,128)(2,1)}, bf16[1,4,2056]{2,1,0:T(4,128)(2,1)S(1)}, u32[]{:S(2)}, u32[]{:S(2)}) collective-permute-start(bf16[1,4,2056]{2,1,0:T(4,128)(2,1)} %get-tuple-element.58), channel_id=1, source_target_pairs={{1,0},{2,1},{3,2},{4,3},{5,4},{6,5},{7,6},{0,7},{9,8},{10,9},{11,1... | collective-permute-start | bytes 49352 | tf_op jit(solution)/shard_map/ppermute | solution.py:22
  216.9 10.6 %rev.13 = bf16[32,16384]{1,0:T(8,128)(2,1)S(1)} reverse(bf16[32,16384]{1,0:T(8,128)(2,1)S(1)} %copy-done), dimensions={1} | reverse | bytes 2097152 | tf_op jit(solution)/shard_map/rev | solution.py:103
  227.6 43.2 %rev.12 = bf16[32,16384]{1,0:T(8,128)(2,1)} reverse(bf16[32,16384]{1,0:T(8,128)(2,1)S(1)} %copy-done.1), dimensions={1} | reverse | bytes 2097152 | tf_op jit(solution)/shard_map/rev | solution.py:103
  270.8 1.4 broadcast_select_fusion.2
  272.3 0.2 fusion.384
  272.5 0.1 collective-permute-start.1
  272.6 2.0 collective-permute-start
  274.6 0.2 fusion.385
  274.9 1.5 collective-permute-done.1
  276.3 2.7 collective-permute-start.3
  279.0 0.1 collective-permute-done
  279.1 0.0 collective-permute-start.2
  279.1 0.1 fusion.376
  279.2 0.9 add_add_fusion.7
  280.0 1.5 fusion.45
  281.5 0.0 collective-permute-done.3
  281.6 0.4 collective-permute-start.4
  281.9 3.6 %collective-permute-done.2 = bf16[1,4,2056]{2,1,0:T(4,128)(2,1)S(1)} collective-permute-done((bf16[1,4,2056]{2,1,0:T(4,128)(2,1)S(1)}, bf16[1,4,2056]{2,1,0:T(4,128)(2,1)S(1)}, u32[]{:S(2)}, u32[]{:S(2)}) %collective-permute-start.2) | collective-permute-done | bytes 16480 | tf_op jit(solution)/shard_map/ppermute | solution.py:21
  285.5 0.1 fusion.377
  285.6 0.9 add_add_fusion.3
  286.5 1.5 fusion.30
  288.0 0.0 collective-permute-done.7
  288.0 0.0 collective-permute-done.6
  288.0 0.1 fusion.379
  288.1 0.9 add_add_fusion
  289.0 1.5 fusion
  290.5 0.0 collective-permute-done.5
  290.5 0.0 collective-permute-done.4
  290.5 0.1 fusion.378
  290.5 0.9 add_add_fusion.1
  291.4 1.5 fusion.15
  292.9 6.8 %fusion.87 = f32[1,32,2048]{2,1,0:T(8,128)S(1)} fusion(f32[35,2051]{1,0:T(8,128)S(1)} %get-tuple-element.38, f32[35,2051]{1,0:T(8,128)S(1)} %get-tuple-element.42, f32[35,2051]{1,0:T(8,128)S(1)} %get-tuple-element.46, f32[35,2051]{1,0:T(8,128)S(1)} %get-tuple-element.50, f32[]{:T(128)} %bitcast.32, f32[]{:T(128)} %bitcast.24, f32[]{:T(128)} %bitcast.16, ...), kind=kLoop, calls=%fused_computation.597 | loop fusion | flops 9633792 | bytes 17041424 | tf_op jit(solution)/shard_map/stack | solution.py:127
  299.7 6.6 %fusion.67 = f32[1,32,2048]{2,1,0:T(8,128)S(1)} fusion(f32[35,2051]{1,0:T(8,128)S(1)} %get-tuple-element.39, f32[35,2051]{1,0:T(8,128)S(1)} %get-tuple-element.43, f32[35,2051]{1,0:T(8,128)S(1)} %get-tuple-element.47, f32[35,2051]{1,0:T(8,128)S(1)} %get-tuple-element.51, f32[]{:T(128)} %bitcast.32, f32[]{:T(128)} %bitcast.24, f32[]{:T(128)} %bitcast.16, ...), kind=kLoop, calls=%fused_computation.577 | loop fusion | flops 9633792 | bytes 17041424 | tf_op jit(solution)/shard_map/stack | solution.py:127
  306.3 0.8 maximum_bitcast_fusion.1
  307.2 6.1 %multiply_subtract_fusion.9 = (f32[32,2048]{1,0:T(8,128)S(1)}, f32[32,2048]{1,0:T(8,128)S(1)}, f32[32,2048]{1,0:T(8,128)S(1)}, f32[32,2048]{1,0:T(8,128)S(1)}, f...) fusion(f32[]{:T(128)} %bitcast.16, f32[]{:T(128)} %bitcast, f32[35,2051]{1,0:T(8,128)S(1)} %get-tuple-element.48, ...), kind=kLoop, calls=%fused_computation.899 | loop fusion | flops 12320768 | bytes 22546440 | tf_op jit(solution)/shard_map/sub | solution.py:95
  313.3 2.8 multiply_subtract_fusion.8
  316.1 1.4 multiply_subtract_fusion.2
  317.5 6.2 %subtract_bitcast_fusion.3 = (f32[1,32,2048]{2,1,0:T(8,128)S(1)}, f32[32,2048]{1,0:T(8,128)S(1)}, f32[32,2048]{1,0:T(8,128)S(1)}, f32[32,2048]{1,0:T(8,128)S(1)}...) fusion(f32[]{:T(128)} %bitcast.32, ...), kind=kLoop, calls=%fused_computation.895 | loop fusion | flops 12451840 | bytes 23595016 | tf_op jit(solution)/shard_map/stack | solution.py:128
  323.7 2.2 subtract_bitcast_fusion.1
  325.9 1.5 subtract_bitcast_fusion.2
  327.4 0.7 subtract_bitcast_fusion
  328.2 1.1 maximum_bitcast_fusion
  (19 shorter events, 0.1 us)
Async XLA Ops:
  7.2 104.3 %all-reduce.3.cloned.1.call-start = ((), (), s32[]{:S(2)}) async-start(), calls=%async_computation | async-start | bytes 8388608 | tf_op jit(solution)/shard_map/psum | solution.py:29
  23.0 0.7 copy-start.4
  23.0 4.0 %copy-start.5 = (s32[1,4]{1,0:T(1,128)S(1)}, s32[1,4]{1,0:T(1,128)}, u32[]{:S(2)}) copy-start(s32[1,4]{1,0:T(1,128)} %param.9) | copy-start | bytes 52
  23.0 7.2 %copy-start.6 = (f32[4]{0:T(128)S(1)}, f32[4]{0:T(128)}, u32[]{:S(2)}) copy-start(f32[4]{0:T(128)} %param.11) | copy-start | bytes 52
  23.0 7.9 %copy-start.7 = (s32[4,16]{1,0:T(4,128)S(1)}, s32[4,16]{1,0:T(4,128)}, u32[]{:S(2)}) copy-start(s32[4,16]{1,0:T(4,128)} %param.10) | copy-start | bytes 772
  111.5 50.0 %copy-start.3 = (bf16[32,16384]{1,0:T(8,128)(2,1)S(1)}, bf16[32,16384]{1,0:T(8,128)(2,1)}, u32[]{:S(2)}) copy-start(bf16[32,16384]{1,0:T(8,128)(2,1)} %get-tuple-element.3) | copy-start | bytes 3145732
  161.5 43.2 %copy-start.2 = (bf16[32,16384]{1,0:T(8,128)(2,1)S(1)}, bf16[32,16384]{1,0:T(8,128)(2,1)}, u32[]{:S(2)}) copy-start(bf16[32,16384]{1,0:T(8,128)(2,1)} %get-tuple-element.2) | copy-start | bytes 3145732
  206.4 10.5 %copy-start = (bf16[32,16384]{1,0:T(8,128)(2,1)S(1)}, bf16[32,16384]{1,0:T(8,128)(2,1)}, u32[]{:S(2)}) copy-start(bf16[32,16384]{1,0:T(8,128)(2,1)} %get-tuple-element.4) | copy-start | bytes 3145732
  207.1 80.9 %collective-permute-start.7 = (bf16[1,4,2056]{2,1,0:T(4,128)(2,1)}, bf16[1,4,2056]{2,1,0:T(4,128)(2,1)S(1)}, u32[]{:S(2)}, u32[]{:S(2)}) collective-permute-start(bf16[1,4,2056]{2,1,0:T(4,128)(2,1)} %get-tuple-element.60), channel_id=1, source_target_pairs={{1,0},{2,1},{3,2},{4,3},{5,4},{6,5},{7,6},{0,7},{9,8},{10,9},{11,1... | collective-permute-start | bytes 49352 | tf_op jit(solution)/shard_map/ppermute | solution.py:22
  211.3 76.7 %collective-permute-start.6 = (bf16[1,4,2056]{2,1,0:T(4,128)(2,1)}, bf16[1,4,2056]{2,1,0:T(4,128)(2,1)S(1)}, u32[]{:S(2)}, u32[]{:S(2)}) collective-permute-start(bf16[1,4,2056]{2,1,0:T(4,128)(2,1)} %get-tuple-element.59), channel_id=1, source_target_pairs={{0,1},{1,2},{2,3},{3,4},{4,5},{5,6},{6,7},{7,0},{8,9},{9,10},{10,1... | collective-permute-start | bytes 49352 | tf_op jit(solution)/shard_map/ppermute | solution.py:21
  211.6 16.0 %copy-start.1 = (bf16[32,16384]{1,0:T(8,128)(2,1)S(1)}, bf16[32,16384]{1,0:T(8,128)(2,1)}, u32[]{:S(2)}) copy-start(bf16[32,16384]{1,0:T(8,128)(2,1)} %get-tuple-element.5) | copy-start | bytes 3145732
  212.2 78.3 %collective-permute-start.5 = (bf16[1,4,2056]{2,1,0:T(4,128)(2,1)}, bf16[1,4,2056]{2,1,0:T(4,128)(2,1)S(1)}, u32[]{:S(2)}, u32[]{:S(2)}) collective-permute-start(bf16[1,4,2056]{2,1,0:T(4,128)(2,1)} %get-tuple-element.58), channel_id=1, source_target_pairs={{1,0},{2,1},{3,2},{4,3},{5,4},{6,5},{7,6},{0,7},{9,8},{10,9},{11,1... | collective-permute-start | bytes 49352 | tf_op jit(solution)/shard_map/ppermute | solution.py:22
  272.5 3.8 %collective-permute-start.1 = (bf16[1,4,2056]{2,1,0:T(4,128)(2,1)S(1)}, bf16[1,4,2056]{2,1,0:T(4,128)(2,1)S(1)}, u32[]{:S(2)}, u32[]{:S(2)}) collective-permute-start(bf16[1,4,2056]{2,1,0:T(4,128)(2,1)S(1)} %get-tuple-element.54), channel_id=1, source_target_pairs={{1,0},{2,1},{3,2},{4,3},{5,4},{6,5},{7,6},{0,7},{9,8},{10,9},{11,1... | collective-permute-start | bytes 49352 | tf_op jit(solution)/shard_map/ppermute | solution.py:22
  272.6 6.5 %collective-permute-start = (bf16[1,4,2056]{2,1,0:T(4,128)(2,1)S(1)}, bf16[1,4,2056]{2,1,0:T(4,128)(2,1)S(1)}, u32[]{:S(2)}, u32[]{:S(2)}) collective-permute-start(bf16[1,4,2056]{2,1,0:T(4,128)(2,1)S(1)} %get-tuple-element.53), channel_id=1, source_target_pairs={{0,1},{1,2},{2,3},{3,4},{4,5},{5,6},{6,7},{7,0},{8,9},{9,10},{10,1... | collective-permute-start | bytes 49352 | tf_op jit(solution)/shard_map/ppermute | solution.py:21
  276.3 5.2 %collective-permute-start.3 = (bf16[1,4,2056]{2,1,0:T(4,128)(2,1)S(1)}, bf16[1,4,2056]{2,1,0:T(4,128)(2,1)S(1)}, u32[]{:S(2)}, u32[]{:S(2)}) collective-permute-start(bf16[1,4,2056]{2,1,0:T(4,128)(2,1)S(1)} %get-tuple-element.56), channel_id=1, source_target_pairs={{1,0},{2,1},{3,2},{4,3},{5,4},{6,5},{7,6},{0,7},{9,8},{10,9},{11,1... | collective-permute-start | bytes 49352 | tf_op jit(solution)/shard_map/ppermute | solution.py:22
  279.1 6.4 %collective-permute-start.2 = (bf16[1,4,2056]{2,1,0:T(4,128)(2,1)S(1)}, bf16[1,4,2056]{2,1,0:T(4,128)(2,1)S(1)}, u32[]{:S(2)}, u32[]{:S(2)}) collective-permute-start(bf16[1,4,2056]{2,1,0:T(4,128)(2,1)S(1)} %get-tuple-element.55), channel_id=1, source_target_pairs={{0,1},{1,2},{2,3},{3,4},{4,5},{5,6},{6,7},{7,0},{8,9},{9,10},{10,1... | collective-permute-start | bytes 49352 | tf_op jit(solution)/shard_map/ppermute | solution.py:21
  281.6 8.9 %collective-permute-start.4 = (bf16[1,4,2056]{2,1,0:T(4,128)(2,1)S(1)}, bf16[1,4,2056]{2,1,0:T(4,128)(2,1)S(1)}, u32[]{:S(2)}, u32[]{:S(2)}) collective-permute-start(bf16[1,4,2056]{2,1,0:T(4,128)(2,1)S(1)} %get-tuple-element.57), channel_id=1, source_target_pairs={{0,1},{1,2},{2,3},{3,4},{4,5},{5,6},{6,7},{7,0},{8,9},{9,10},{10,1... | collective-permute-start | bytes 49352 | tf_op jit(solution)/shard_map/ppermute | solution.py:21
Sparse Core Ops, SparseCore 0:
  23.2 88.2 all-reduce.2
where the time goes:
time: 340 us; the launch traced here: 336 us
  local copies, waits for them, and re-layouts  152 us (45%)
  waiting for transfers between devices  85.7 us (25%)
  other arithmetic  54 us (16%)
  between operations  29.7 us (9%)
  starting transfers between devices  14.2 us (4%)
    rev x4, local copies, waits for them, and re-layouts, cut_columns(): flipped = jnp.where(flip == 1, band[..., ::-1], band)  147 us
    psum x1, waiting for transfers between devices, spread(): return lax.psum(kept, axis)  80.6 us
    another operation x2, other arithmetic, body(): deflect = jnp.stack([state[0], state[1]])[:, None]  13.4 us
    ppermute x4, starting transfers between devices, extended_2(): after = lax.ppermute(first, axis, down)  11.7 us
    another operation x4, other arithmetic, body(): distort = jnp.stack([state[2], state[3], state[4], state[5]])[:, None]  10.6 us
  transfers between devices with their start and end apart: 9, of which 4 were waited for; matrix products, arithmetic and copies ran while one was open for 20% of the time, Pallas kernels for 0%

commit v1 on v0

--- a/solution.py
+++ b/solution.py
@@ -26,7 +26,7 @@
 
 def spread(value, axis, source):
     kept = jnp.where(lax.axis_index(axis) == source, value, 0).astype(value.dtype)
-    return lax.psum(kept, axis)
+    return jnp.sum(lax.all_gather(kept, axis), axis=0)
 
 
 def cubic_weights(frac):

time: 340 us -> 245 us (0.72); the launches traced: 336 us -> 245 us
  local copies, waits for them, and re-layouts: 152 us -> 46.2 us
  other arithmetic: 54 us -> 63 us
  starting transfers between devices: 14.2 us -> 20.4 us
    rev x4, local copies, waits for them, and re-layouts: 147 us -> 42.6 us  [cut_columns(): flipped = jnp.where(flip == 1, band[..., ::-1], band)]
    all_gather x0 -> x4, waiting for transfers between devices: none -> 83.5 us  [spread(): return jnp.sum(lax.all_gather(kept, axis), axis=0)]
    psum x1 -> x0, waiting for transfers between devices: 80.6 us -> none  [spread(): return lax.psum(kept, axis)]
    reduce_sum x0 -> x4, other arithmetic: none -> 11.9 us  [spread(): return jnp.sum(lax.all_gather(kept, axis), axis=0)]
    ppermute x4, starting transfers between devices: 11.7 us -> 15.7 us  [extended_2(): after = lax.ppermute(first, axis, down)]
    ppermute x4, waiting for transfers between devices: 3.65 us -> 0.01 us  [extended_2(): before = lax.ppermute(last, axis, up)]
  transfers between devices with their start and end apart: 9 -> 12, of which waited for: 4 -> 4; matrix products, arithmetic and copies ran while one was open for 20% -> 27% of each run, Pallas kernels for 0% -> 0%
where the time goes in v1:
time: 245 us
  waiting for transfers between devices  85.5 us (35%)
  other arithmetic  63 us (26%)
  local copies, waits for them, and re-layouts  46.2 us (19%)
  between operations  29.7 us (12%)
  starting transfers between devices  20.4 us (8%)
    all_gather x4, waiting for transfers between devices, spread(): return jnp.sum(lax.all_gather(kept, axis), axis=0)  83.5 us
    rev x4, local copies, waits for them, and re-layouts, cut_columns(): flipped = jnp.where(flip == 1, band[..., ::-1], band)  42.6 us
    ppermute x4, starting transfers between devices, extended_2(): after = lax.ppermute(first, axis, down)  15.7 us
    another operation x2, other arithmetic, body(): deflect = jnp.stack([state[0], state[1]])[:, None]  13.2 us
    reduce_sum x4, other arithmetic, spread(): return jnp.sum(lax.all_gather(kept, axis), axis=0)  11.9 us
    another operation x4, other arithmetic, body(): distort = jnp.stack([state[2], state[3], state[4], state[5]])[:, None]  10.1 us
    sub x1, other arithmetic, advance(): new_11 = a_11 - lens * (hess_xx * a_11 + hess_xy * a_21)  6.12 us
    add x4, other arithmetic, derivatives(): sum((first_coef[p] * first_coef[q] * window(p - 2, q - 2) for p in range(...  6 us
  transfers between devices with their start and end apart: 12, of which 4 were waited for; matrix products, arithmetic and copies ran while one was open for 27% of the time, Pallas kernels for 0%

profile of v1, /device:TPU:0, one launch (start us, length us, event | category | flops | bytes accessed | tf_op | source)
XLA Modules:
  0.0 244.7 jit_solution(12625510045282072229)
XLA Ops:
  7.2 0.0 all-gather.9.cloned.1.call-start
  7.2 1.5 fusion.435
  18.9 4.3 %dynamic-slice_select_fusion.3 = (bf16[1,32,16384]{2,1,0:T(8,128)(2,1)}, bf16[1,32,16384]{2,1,0:T(8,128)(2,1)}, bf16[1,32,16384]{2,1,0:T(8,128)(2,1)}, bf16[1,32,16384]{2,1,0:T(8,128)(2,1)}) fusion(bf16[2,32,16384]{2,1,0:T(8,128)(2,1)} %param.6, s32[]{:T(128)S(6)} %select_n.146, pred[]{:T(512)S(6)} %eq.49, s32[]{:T(128)S(6)} %select_n.155, pred[]{:T(512)S(6)} %eq.52, ...), kind=kLoop, calls=%fused_computation.412 | loop fusion | flops 2097152 | bytes 8388628 | tf_op jit(solution)/shard_map/jit(_where)/select_n | solution.py:28
  23.2 0.0 all-gather.9.cloned.1.call-update
  23.3 0.0 all-gather.11.cloned.1.call-start
  23.3 0.7 all-gather.11.cloned.1.call-update
  24.0 0.0 copy-start.1
  24.1 0.0 all-gather.7.cloned.1.call-start
  24.1 0.7 all-gather.7.cloned.1.call-update
  24.8 0.0 all-gather.5.cloned.1.call-start
  24.8 0.5 all-gather.5.cloned.1.call-update
  25.4 0.7 fusion.436
  28.7 0.7 fusion.434
  32.0 0.6 fusion.433
  32.7 27.9 %all-gather.9.cloned.1.call-done = bf16[4,32,16384]{2,1,0:T(8,128)(2,1)} async-done(((bf16[1,32,16384]{2,1,0:T(8,128)(2,1)}), bf16[4,32,16384]{2,1,0:T(8,128)(2,1)}) %all-gather.9.cloned.1.call-update) | async-done | bytes 4194320 | tf_op jit(solution)/shard_map/all_gather | solution.py:29
  60.6 3.0 %reduce_sum.50 = bf16[32,16384]{1,0:T(8,128)(2,1)S(1)} reduce(bf16[4,32,16384]{2,1,0:T(8,128)(2,1)} %all-gather.9.cloned.1.call-done, bf16[]{:T(256)} %constant.163.clone.1), dimensions={0}, to_apply=%region_2.3 | reduce | flops 1572864 | bytes 5242882 | tf_op jit(solution)/shard_map/reduce_sum | solution.py:29
  63.6 10.7 %rev.14 = bf16[32,16384]{1,0:T(8,128)(2,1)S(1)} reverse(bf16[32,16384]{1,0:T(8,128)(2,1)S(1)} %reduce_sum.50), dimensions={1} | reverse | bytes 2097152 | tf_op jit(solution)/shard_map/rev | solution.py:103
  74.2 0.1 broadcast_select_fusion.1
  74.4 0.2 fusion.386
  74.6 1.5 collective-permute-start.4
  76.2 3.2 %collective-permute-start.5 = (bf16[1,4,2056]{2,1,0:T(4,128)(2,1)S(1)}, bf16[1,4,2056]{2,1,0:T(4,128)(2,1)S(1)}, u32[]{:S(2)}, u32[]{:S(2)}) collective-permute-start(bf16[1,4,2056]{2,1,0:T(4,128)(2,1)S(1)} %get-tuple-element.54), channel_id=1, source_target_pairs={{1,0},{2,1},{3,2},{4,3},{5,4},{6,5},{7,6},{0,7},{9,8},{10,9},{11,1... | collective-permute-start | bytes 49352 | tf_op jit(solution)/shard_map/ppermute | solution.py:22
  79.4 17.3 %all-gather.11.cloned.1.call-done = bf16[4,32,16384]{2,1,0:T(8,128)(2,1)} async-done(((bf16[1,32,16384]{2,1,0:T(8,128)(2,1)}), bf16[4,32,16384]{2,1,0:T(8,128)(2,1)}) %all-gather.11.cloned.1.call-update) | async-done | bytes 4194320 | tf_op jit(solution)/shard_map/all_gather | solution.py:29
  96.7 3.0 %reduce_sum.51 = bf16[32,16384]{1,0:T(8,128)(2,1)S(1)} reduce(bf16[4,32,16384]{2,1,0:T(8,128)(2,1)} %all-gather.11.cloned.1.call-done, bf16[]{:T(256)} %constant.163.clone.1), dimensions={0}, to_apply=%region_3.4 | reduce | flops 1572864 | bytes 5242882 | tf_op jit(solution)/shard_map/reduce_sum | solution.py:29
  99.7 10.7 %rev.15 = bf16[32,16384]{1,0:T(8,128)(2,1)S(1)} reverse(bf16[32,16384]{1,0:T(8,128)(2,1)S(1)} %reduce_sum.51), dimensions={1} | reverse | bytes 2097152 | tf_op jit(solution)/shard_map/rev | solution.py:103
  110.4 0.1 broadcast_select_fusion
  110.5 0.2 fusion.387
  110.8 1.5 collective-permute-start.6
  112.3 3.3 %collective-permute-start.7 = (bf16[1,4,2056]{2,1,0:T(4,128)(2,1)S(1)}, bf16[1,4,2056]{2,1,0:T(4,128)(2,1)S(1)}, u32[]{:S(2)}, u32[]{:S(2)}) collective-permute-start(bf16[1,4,2056]{2,1,0:T(4,128)(2,1)S(1)} %get-tuple-element.56), channel_id=1, source_target_pairs={{1,0},{2,1},{3,2},{4,3},{5,4},{6,5},{7,6},{0,7},{9,8},{10,9},{11,1... | collective-permute-start | bytes 49352 | tf_op jit(solution)/shard_map/ppermute | solution.py:22
  115.6 17.3 %all-gather.7.cloned.1.call-done = bf16[4,32,16384]{2,1,0:T(8,128)(2,1)} async-done(((bf16[1,32,16384]{2,1,0:T(8,128)(2,1)}), bf16[4,32,16384]{2,1,0:T(8,128)(2,1)}) %all-gather.7.cloned.1.call-update) | async-done | bytes 4194320 | tf_op jit(solution)/shard_map/all_gather | solution.py:29
  132.8 3.0 %reduce_sum.49 = bf16[32,16384]{1,0:T(8,128)(2,1)S(1)} reduce(bf16[4,32,16384]{2,1,0:T(8,128)(2,1)} %all-gather.7.cloned.1.call-done, bf16[]{:T(256)} %constant.163.clone.1), dimensions={0}, to_apply=%region_1.2 | reduce | flops 1572864 | bytes 5242882 | tf_op jit(solution)/shard_map/reduce_sum | solution.py:29
  135.8 10.7 %rev.13 = bf16[32,16384]{1,0:T(8,128)(2,1)S(1)} reverse(bf16[32,16384]{1,0:T(8,128)(2,1)S(1)} %reduce_sum.49), dimensions={1} | reverse | bytes 2097152 | tf_op jit(solution)/shard_map/rev | solution.py:103
  146.5 0.1 broadcast_select_fusion.2
  146.6 0.2 fusion.385
  146.9 1.5 collective-permute-start.2
  148.3 21.1 %all-gather.5.cloned.1.call-done = bf16[4,32,16384]{2,1,0:T(8,128)(2,1)} async-done(((bf16[1,32,16384]{2,1,0:T(8,128)(2,1)}), bf16[4,32,16384]{2,1,0:T(8,128)(2,1)}) %all-gather.5.cloned.1.call-update) | async-done | bytes 4194320 | tf_op jit(solution)/shard_map/all_gather | solution.py:29
  169.4 3.0 %reduce_sum.48 = bf16[32,16384]{1,0:T(8,128)(2,1)S(1)} reduce(bf16[4,32,16384]{2,1,0:T(8,128)(2,1)} %all-gather.5.cloned.1.call-done, bf16[]{:T(256)} %constant.163.clone.1), dimensions={0}, to_apply=%region_0.1 | reduce | flops 1572864 | bytes 5242882 | tf_op jit(solution)/shard_map/reduce_sum | solution.py:29
  172.4 10.7 %rev.12 = bf16[32,16384]{1,0:T(8,128)(2,1)S(1)} reverse(bf16[32,16384]{1,0:T(8,128)(2,1)S(1)} %reduce_sum.48), dimensions={1} | reverse | bytes 2097152 | tf_op jit(solution)/shard_map/rev | solution.py:103
  183.0 0.1 broadcast_select_fusion.3
  183.2 0.2 fusion.384
  183.4 4.3 %collective-permute-start.3 = (bf16[1,4,2056]{2,1,0:T(4,128)(2,1)S(1)}, bf16[1,4,2056]{2,1,0:T(4,128)(2,1)S(1)}, u32[]{:S(2)}, u32[]{:S(2)}) collective-permute-start(bf16[1,4,2056]{2,1,0:T(4,128)(2,1)S(1)} %get-tuple-element.52), channel_id=1, source_target_pairs={{1,0},{2,1},{3,2},{4,3},{5,4},{6,5},{7,6},{0,7},{9,8},{10,9},{11,1... | collective-permute-start | bytes 49352 | tf_op jit(solution)/shard_map/ppermute | solution.py:22
  187.7 0.1 fusion.378
  187.8 0.9 add_add_fusion.1
  188.6 1.5 fusion.15
  190.2 5.0 %collective-permute-start.1 = (bf16[1,4,2056]{2,1,0:T(4,128)(2,1)S(1)}, bf16[1,4,2056]{2,1,0:T(4,128)(2,1)S(1)}, u32[]{:S(2)}, u32[]{:S(2)}) collective-permute-start(bf16[1,4,2056]{2,1,0:T(4,128)(2,1)S(1)} %get-tuple-element.50), channel_id=1, source_target_pairs={{1,0},{2,1},{3,2},{4,3},{5,4},{6,5},{7,6},{0,7},{9,8},{10,9},{11,1... | collective-permute-start | bytes 49352 | tf_op jit(solution)/shard_map/ppermute | solution.py:22
  195.1 0.1 fusion.379
  195.2 0.9 add_add_fusion
  196.1 1.5 fusion
  197.6 0.1 fusion.377
  197.6 0.9 add_add_fusion.3
  198.5 1.5 fusion.30
  200.1 0.1 fusion.376
  200.1 1.5 fusion.45
  201.6 0.9 add_add_fusion.7
  202.5 6.7 %fusion.67 = f32[1,32,2048]{2,1,0:T(8,128)S(1)} fusion(f32[35,2051]{1,0:T(8,128)S(1)} %get-tuple-element.35, f32[35,2051]{1,0:T(8,128)S(1)} %get-tuple-element.39, f32[35,2051]{1,0:T(8,128)S(1)} %get-tuple-element.43, f32[35,2051]{1,0:T(8,128)S(1)} %get-tuple-element.47, f32[]{:T(128)} %bitcast.29, f32[]{:T(128)} %bitcast.22, f32[]{:T(128)} %bitcast.15, ...), kind=kLoop, calls=%fused_computation.577 | loop fusion | flops 9633792 | bytes 17041424 | tf_op jit(solution)/shard_map/stack | solution.py:127
  209.2 6.5 %fusion.87 = f32[1,32,2048]{2,1,0:T(8,128)S(1)} fusion(f32[35,2051]{1,0:T(8,128)S(1)} %get-tuple-element.34, f32[35,2051]{1,0:T(8,128)S(1)} %get-tuple-element.38, f32[35,2051]{1,0:T(8,128)S(1)} %get-tuple-element.42, f32[35,2051]{1,0:T(8,128)S(1)} %get-tuple-element.46, f32[]{:T(128)} %bitcast.29, f32[]{:T(128)} %bitcast.22, f32[]{:T(128)} %bitcast.15, ...), kind=kLoop, calls=%fused_computation.597 | loop fusion | flops 9633792 | bytes 17041424 | tf_op jit(solution)/shard_map/stack | solution.py:127
  215.7 0.8 maximum_bitcast_fusion.1
  216.5 6.1 %multiply_subtract_fusion.9 = (f32[32,2048]{1,0:T(8,128)S(1)}, f32[32,2048]{1,0:T(8,128)S(1)}, f32[32,2048]{1,0:T(8,128)S(1)}, f32[32,2048]{1,0:T(8,128)S(1)}, f...) fusion(f32[]{:T(128)} %bitcast.15, f32[]{:T(128)} %bitcast, f32[35,2051]{1,0:T(8,128)S(1)} %get-tuple-element.44, ...), kind=kLoop, calls=%fused_computation.899 | loop fusion | flops 12320768 | bytes 22546440 | tf_op jit(solution)/shard_map/sub | solution.py:95
  222.7 2.9 %multiply_subtract_fusion.8 = (f32[32,2048]{1,0:T(8,128)S(1)}, f32[32,2048]{1,0:T(8,128)S(1)}) fusion(f32[32,2048]{1,0:T(8,128)S(1)} %get-tuple-element.20, f32[]{:T(128)} %bitcast.15, f32[32,2048]{1,0:T(8,128)S(1)} %get-tuple-element.18, f32[32,2048]{1,0:T(8,128)S(1)} %get-tuple-element.19, f32[]{:T(128)} %bitcast, f32[32,2048]{1,0:T(8,128)S(1)} %get-tuple-element.17, ...), kind=kLoop, calls=%fused_computation.898 | loop fusion | flops 3145728 | bytes 5769224 | tf_op jit(solution)/shard_map/sub | solution.py:97
  225.5 1.5 multiply_subtract_fusion.2
  227.0 6.0 %subtract_bitcast_fusion.3 = (f32[1,32,2048]{2,1,0:T(8,128)S(1)}, f32[32,2048]{1,0:T(8,128)S(1)}, f32[32,2048]{1,0:T(8,128)S(1)}, f32[32,2048]{1,0:T(8,128)S(1)}...) fusion(f32[]{:T(128)} %bitcast.29, ...), kind=kLoop, calls=%fused_computation.895 | loop fusion | flops 12451840 | bytes 23595016 | tf_op jit(solution)/shard_map/stack | solution.py:128
  233.0 2.1 subtract_bitcast_fusion.1
  235.1 1.3 subtract_bitcast_fusion.2
  236.5 0.6 subtract_bitcast_fusion
  237.1 1.0 maximum_bitcast_fusion
  (26 shorter events, 0.2 us)
Async XLA Ops:
  7.2 53.4 %all-gather.9.cloned.1.call-start = ((), (), s32[]{:S(2)}) async-start(), calls=%async_computation.2 | async-start | bytes 5242880 | tf_op jit(solution)/shard_map/all_gather | solution.py:29
  23.3 73.5 %all-gather.11.cloned.1.call-start = ((), (), s32[]{:S(2)}) async-start(), calls=%async_computation.3 | async-start | bytes 5242880 | tf_op jit(solution)/shard_map/all_gather | solution.py:29
  24.0 1.4 copy-start
  24.0 4.7 %copy-start.1 = (s32[1,4]{1,0:T(1,128)S(1)}, s32[1,4]{1,0:T(1,128)}, u32[]{:S(2)}) copy-start(s32[1,4]{1,0:T(1,128)} %param.9) | copy-start | bytes 52
  24.0 8.0 %copy-start.2 = (f32[4]{0:T(128)S(1)}, f32[4]{0:T(128)}, u32[]{:S(2)}) copy-start(f32[4]{0:T(128)} %param.11) | copy-start | bytes 52
  24.0 8.6 %copy-start.3 = (s32[4,16]{1,0:T(4,128)S(1)}, s32[4,16]{1,0:T(4,128)}, u32[]{:S(2)}) copy-start(s32[4,16]{1,0:T(4,128)} %param.10) | copy-start | bytes 772
  24.1 108.8 %all-gather.7.cloned.1.call-start = ((), (), s32[]{:S(2)}) async-start(), calls=%async_computation.1 | async-start | bytes 5242880 | tf_op jit(solution)/shard_map/all_gather | solution.py:29
  24.8 144.6 %all-gather.5.cloned.1.call-start = ((), (), s32[]{:S(2)}) async-start(), calls=%async_computation | async-start | bytes 5242880 | tf_op jit(solution)/shard_map/all_gather | solution.py:29
  74.6 108.8 %collective-permute-start.4 = (bf16[1,4,2056]{2,1,0:T(4,128)(2,1)S(1)}, bf16[1,4,2056]{2,1,0:T(4,128)(2,1)S(1)}, u32[]{:S(2)}, u32[]{:S(2)}) collective-permute-start(bf16[1,4,2056]{2,1,0:T(4,128)(2,1)S(1)} %get-tuple-element.53), channel_id=1, source_target_pairs={{0,1},{1,2},{2,3},{3,4},{4,5},{5,6},{6,7},{7,0},{8,9},{9,10},{10,1... | collective-permute-start | bytes 49352 | tf_op jit(solution)/shard_map/ppermute | solution.py:21
  76.2 111.5 %collective-permute-start.5 = (bf16[1,4,2056]{2,1,0:T(4,128)(2,1)S(1)}, bf16[1,4,2056]{2,1,0:T(4,128)(2,1)S(1)}, u32[]{:S(2)}, u32[]{:S(2)}) collective-permute-start(bf16[1,4,2056]{2,1,0:T(4,128)(2,1)S(1)} %get-tuple-element.54), channel_id=1, source_target_pairs={{1,0},{2,1},{3,2},{4,3},{5,4},{6,5},{7,6},{0,7},{9,8},{10,9},{11,1... | collective-permute-start | bytes 49352 | tf_op jit(solution)/shard_map/ppermute | solution.py:22
  110.8 79.4 %collective-permute-start.6 = (bf16[1,4,2056]{2,1,0:T(4,128)(2,1)S(1)}, bf16[1,4,2056]{2,1,0:T(4,128)(2,1)S(1)}, u32[]{:S(2)}, u32[]{:S(2)}) collective-permute-start(bf16[1,4,2056]{2,1,0:T(4,128)(2,1)S(1)} %get-tuple-element.55), channel_id=1, source_target_pairs={{0,1},{1,2},{2,3},{3,4},{4,5},{5,6},{6,7},{7,0},{8,9},{9,10},{10,1... | collective-permute-start | bytes 49352 | tf_op jit(solution)/shard_map/ppermute | solution.py:21
  112.3 82.8 %collective-permute-start.7 = (bf16[1,4,2056]{2,1,0:T(4,128)(2,1)S(1)}, bf16[1,4,2056]{2,1,0:T(4,128)(2,1)S(1)}, u32[]{:S(2)}, u32[]{:S(2)}) collective-permute-start(bf16[1,4,2056]{2,1,0:T(4,128)(2,1)S(1)} %get-tuple-element.56), channel_id=1, source_target_pairs={{1,0},{2,1},{3,2},{4,3},{5,4},{6,5},{7,6},{0,7},{9,8},{10,9},{11,1... | collective-permute-start | bytes 49352 | tf_op jit(solution)/shard_map/ppermute | solution.py:22
  146.9 50.7 %collective-permute-start.2 = (bf16[1,4,2056]{2,1,0:T(4,128)(2,1)S(1)}, bf16[1,4,2056]{2,1,0:T(4,128)(2,1)S(1)}, u32[]{:S(2)}, u32[]{:S(2)}) collective-permute-start(bf16[1,4,2056]{2,1,0:T(4,128)(2,1)S(1)} %get-tuple-element.51), channel_id=1, source_target_pairs={{0,1},{1,2},{2,3},{3,4},{4,5},{5,6},{6,7},{7,0},{8,9},{9,10},{10,1... | collective-permute-start | bytes 49352 | tf_op jit(solution)/shard_map/ppermute | solution.py:21
  183.4 14.1 %collective-permute-start.3 = (bf16[1,4,2056]{2,1,0:T(4,128)(2,1)S(1)}, bf16[1,4,2056]{2,1,0:T(4,128)(2,1)S(1)}, u32[]{:S(2)}, u32[]{:S(2)}) collective-permute-start(bf16[1,4,2056]{2,1,0:T(4,128)(2,1)S(1)} %get-tuple-element.52), channel_id=1, source_target_pairs={{1,0},{2,1},{3,2},{4,3},{5,4},{6,5},{7,6},{0,7},{9,8},{10,9},{11,1... | collective-permute-start | bytes 49352 | tf_op jit(solution)/shard_map/ppermute | solution.py:22
  187.7 12.3 %collective-permute-start = (bf16[1,4,2056]{2,1,0:T(4,128)(2,1)S(1)}, bf16[1,4,2056]{2,1,0:T(4,128)(2,1)S(1)}, u32[]{:S(2)}, u32[]{:S(2)}) collective-permute-start(bf16[1,4,2056]{2,1,0:T(4,128)(2,1)S(1)} %get-tuple-element.49), channel_id=1, source_target_pairs={{0,1},{1,2},{2,3},{3,4},{4,5},{5,6},{6,7},{7,0},{8,9},{9,10},{10,1... | collective-permute-start | bytes 49352 | tf_op jit(solution)/shard_map/ppermute | solution.py:21
  190.2 9.9 %collective-permute-start.1 = (bf16[1,4,2056]{2,1,0:T(4,128)(2,1)S(1)}, bf16[1,4,2056]{2,1,0:T(4,128)(2,1)S(1)}, u32[]{:S(2)}, u32[]{:S(2)}) collective-permute-start(bf16[1,4,2056]{2,1,0:T(4,128)(2,1)S(1)} %get-tuple-element.50), channel_id=1, source_target_pairs={{1,0},{2,1},{3,2},{4,3},{5,4},{6,5},{7,6},{0,7},{9,8},{10,9},{11,1... | collective-permute-start | bytes 49352 | tf_op jit(solution)/shard_map/ppermute | solution.py:22
Sparse Core Ops, SparseCore 0:
  23.4 37.1 all-gather.8
  62.2 34.5 all-gather.10
  98.3 34.4 all-gather.6
  134.8 34.5 all-gather.4
